TPU v7x, 32 devices: a whole 2x2x4 slice. The times are simulated.
32 devices in a mesh: seq: 8 (over z, x), exp: 4 (over y, core).
Axes of the slice: x: 2, y: 2, z: 4, core: 2. Of those that a mesh axis runs over, the one named last changes fastest.
Arguments:
- projected: bfloat16 [4, 1024, 3, 4096], P('exp', 'seq'), may hold values from -8 to 8
- patches: bfloat16 [4, 1024, 4096], P('exp', 'seq'), may hold values from -6 to 6
- norm_gain: float32 [4096], replicated, may hold values from 0.1 to 1.9
- expert_ids: int32 [4, 1024, 2], P('exp', 'seq'), may hold values from 0 to 31, all different within a row; in each aligned block of 128 rows (0 to 127, 128 to 255, ..., all dimensions but the last counted through in order) at most 16 rows name the same one
- gate_levels: int32 [4, 1024, 2], P('exp', 'seq'), may hold values from 1 to 256
- w_gate: bfloat16 [32, 4096, 768], P(('seq', 'exp')), may hold values from -0.09375 to 0.09375
- w_up: bfloat16 [32, 4096, 768], P(('seq', 'exp')), may hold values from -0.09375 to 0.09375
- w_down: bfloat16 [32, 768, 4096], P(('seq', 'exp')), may hold values from -0.21875 to 0.21875
Outputs:
- attended: bfloat16 [4, 1024, 4096], P('exp', 'seq')
- layer_out: bfloat16 [4, 1024, 4096], P('exp', 'seq')
Inputs may be any that keep to these rules, and one draw needn't show every extreme that they name: `expert_ids`: each patch names two different experts. Among the 128 patches of one device (aligned blocks of rows, sequences first), at most 16 name the same expert, and in every draw some expert is named by exactly 16 patches of some device.
All inputs are finite; a program needn't handle non-finite values.
Results may differ from a plain program's by a relative error of at most 0.0068.
Values may be sent and summed in bfloat16 or wider, within the bound.
No kernel may reach another device: no remote copies, remote signals or barrier semaphores. Data moves between devices by JAX's collectives and lax.ppermute only.
A program may use at most 128 MiB of HBM per device.

v0:
```python
import math
import jax
import jax.numpy as jnp
from jax import lax
from jax.sharding import PartitionSpec as P

HEADS = 32


def expert_ffn(arrived, w_gate, w_up, w_down):
    flat_rows = arrived.reshape(-1, arrived.shape[-1])
    gate_part = jnp.dot(flat_rows, w_gate[0], preferred_element_type=jnp.float32)
    up_part = jnp.dot(flat_rows, w_up[0], preferred_element_type=jnp.float32)
    hidden = (jax.nn.silu(gate_part) * up_part).astype(jnp.bfloat16)
    result = jnp.dot(hidden, w_down[0], preferred_element_type=jnp.float32).astype(jnp.bfloat16)
    return result.reshape(arrived.shape[:-1] + (w_down.shape[2],))


def shards(projected, patches, norm_gain, expert_ids, gate_levels, w_gate, w_up, w_down):
    seq_count = lax.axis_size("seq")
    exp_count = lax.axis_size("exp")
    tok_rows = patches.shape[1]
    width = patches.shape[2]
    regrouped = lax.all_to_all(projected, "seq", split_axis=3, concat_axis=1, tiled=True)
    length = regrouped.shape[1]
    local_width = regrouped.shape[3]
    local_heads = HEADS // seq_count
    head_width = local_width // local_heads
    scale = 1.0 / math.sqrt(head_width)
    query_rows = regrouped[0, :, 0].reshape(length, local_heads, head_width)
    key_rows = regrouped[0, :, 1].reshape(length, local_heads, head_width)
    value_rows = regrouped[0, :, 2].reshape(length, local_heads, head_width)
    step_rows = min(512, length)

    def attend(block_index):
        start = block_index * step_rows
        query_part = lax.dynamic_slice_in_dim(query_rows, start, step_rows, 0)
        scores = (
            jnp.einsum("qhd,khd->hqk", query_part, key_rows, preferred_element_type=jnp.float32)
            * scale
        )
        query_pos = start + lax.broadcasted_iota(jnp.int32, (step_rows, length), 0)
        key_pos = lax.broadcasted_iota(jnp.int32, (step_rows, length), 1)
        scores = jnp.where((key_pos <= query_pos)[None], scores, jnp.float32(-1e30))
        highest = jnp.max(scores, axis=-1, keepdims=True)
        weights = jnp.exp(scores - highest)
        probs = (weights / jnp.sum(weights, axis=-1, keepdims=True)).astype(jnp.bfloat16)
        mixed_part = jnp.einsum(
            "hqk,khd->qhd", probs, value_rows, preferred_element_type=jnp.float32
        )
        return mixed_part.astype(jnp.bfloat16).reshape(step_rows, local_width)

    outputs = lax.map(attend, jnp.arange(length // step_rows, dtype=jnp.int32))
    head_major = outputs.reshape(1, length, local_width)
    attended = lax.all_to_all(head_major, "seq", split_axis=1, concat_axis=2, tiled=True)
    stream = (patches.astype(jnp.float32) + attended.astype(jnp.float32)).astype(jnp.bfloat16)
    stream_f = stream.astype(jnp.float32)
    mean_square = jnp.mean(stream_f * stream_f, axis=-1, keepdims=True)
    normed = (stream_f * lax.rsqrt(mean_square + 1e-05) * norm_gain).astype(jnp.bfloat16)
    normed_rows = normed[0]
    expert_count = seq_count * exp_count * w_gate.shape[0]
    capacity = max(2, 4 * tok_rows // expert_count)
    routed = expert_ids[0].reshape(-1)
    onehot = (routed[:, None] == jnp.arange(expert_count, dtype=jnp.int32)[None, :]).astype(
        jnp.int32
    )
    slot = jnp.sum(jnp.cumsum(onehot, axis=0) * onehot, axis=1) - 1
    position = routed * capacity + slot
    selection = jnp.arange(expert_count * capacity, dtype=jnp.int32)[:, None] == position[None, :]
    dispatch_matrix = jnp.any(
        selection.reshape(expert_count * capacity, tok_rows, 2), axis=2
    ).astype(jnp.bfloat16)
    buffer = jnp.dot(dispatch_matrix, normed_rows, preferred_element_type=jnp.float32).astype(
        jnp.bfloat16
    )
    outgoing = buffer.reshape(expert_count, capacity, width)
    processed = expert_ffn(
        lax.all_to_all(outgoing, ("seq", "exp"), split_axis=0, concat_axis=0, tiled=True),
        w_gate,
        w_up,
        w_down,
    )
    returned = lax.all_to_all(processed, ("seq", "exp"), split_axis=0, concat_axis=0, tiled=True)
    flat_back = returned.reshape(expert_count * capacity, width)
    picked = flat_back[position].reshape(tok_rows, 2, width).astype(jnp.float32)
    levels = gate_levels[0].astype(jnp.float32)
    share = levels / jnp.sum(levels, axis=-1, keepdims=True)
    mixture = picked[:, 0, :] * share[:, 0:1] + picked[:, 1, :] * share[:, 1:2]
    layer_out = (stream_f[0] + mixture).astype(jnp.bfloat16)
    return (attended, layer_out[None])


def solution(mesh):
    return jax.shard_map(
        shards,
        mesh=mesh,
        in_specs=(
            P("exp", "seq", None, None),
            P("exp", "seq", None),
            P(),
            P("exp", "seq", None),
            P("exp", "seq", None),
            P(("seq", "exp"), None, None),
            P(("seq", "exp"), None, None),
            P(("seq", "exp"), None, None),
        ),
        out_specs=(P("exp", "seq", None), P("exp", "seq", None)),
        check_vma=False,
    )
```

profile of v0, /device:TPU:0, one launch (start us, length us, event | category | flops | bytes accessed | tf_op | source)
XLA Modules:
  0.0 452.3 jit_solution(14695792651133212737)
XLA Ops:
  0.6 7.2 %copy.54 = bf16[1,128,3,4096]{1,2,0,3:T(4,128)(2,1)} copy(bf16[1,128,3,4096]{3,1,2,0:T(8,128)(2,1)} %param.10) | data formatting | bytes 6291456 | tf_op args[0]
  7.8 7.3 %all-to-all-start = ((bf16[1,128,3,4096]{1,2,0,3:T(4,128)(2,1)}), bf16[1,128,3,4096]{1,2,0,3:T(4,128)(2,1)}, u32[]{:S(2)}, u32[]{:S(2)}) async-start(bf16[1,128,3,4096]{1,2,0,3:T(4,128)(2,1)} %copy.54), calls=%async_computation | async-start | bytes 8388608 | tf_op jit(solution)/shard_map/all_to_all | solution.py:24
  15.1 93.3 %all-to-all-done = bf16[1,128,3,4096]{1,2,0,3:T(4,128)(2,1)} async-done(((bf16[1,128,3,4096]{1,2,0,3:T(4,128)(2,1)}), bf16[1,128,3,4096]{1,2,0,3:T(4,128)(2,1)}, u32[]{:S(2)}, u32[]{:S(2)}) %all-to-all-start) | async-done | bytes 3145760 | tf_op jit(solution)/shard_map/all_to_all | solution.py:24
  108.4 4.8 %copy.81 = bf16[1,128,3,8,512]{1,3,4,2,0:T(8,128)(2,1)S(1)} copy(bf16[1,128,3,8,512]{1,2,4,3,0:T(4,128)(2,1)} %bitcast.3) | data formatting | bytes 6291456 | tf_op jit(solution)/shard_map/all_to_all | solution.py:24
  113.1 3.4 all_to_all.35
  116.5 3.8 fusion.55
  120.3 0.7 copy.57
  120.9 0.0 copy-done.1
  120.9 29.8 %while.10 = (s32[]{:T(128)}, bf16[2,512,512]{2,1,0:T(8,128)(2,1)S(1)}, s32[2]{0:T(128)S(1)}, bf16[1024,4,128]{0,2,1:T(8,128)(2,1)}, bf16[1024,4,128]{2,0,1:T(8,1...) while((s32[]{:T(128)}, ...), condition=%wide.region_3.4_spmd, body=%wide.region_0.3_spmd.sunk | while | flops 1087112704 | bytes 23089332 | solution.py:53
  120.9 0.6 dynamic_slice.22
  122.2 0.4 iota_compare_fusion.5
  122.6 7.5 %fusion.70 = (f32[4,512]{1,0:T(4,128)S(1)}, f32[4,512,1024]{2,1,0:T(8,128)}) fusion(pred[512,1024]{1,0:T(8,128)(4,1)S(1)} %iota_compare_fusion.5, bf16[1024,4,128]{2,0,1:T(8,128)(2,1)S(1)} %get-tuple-element.153, bf16[1024,4,128]{0,2,1:T(8,128)(2,1)} %get-tuple-element.152, s32[]{:T(128)S(6)} %select_n.32), kind=kOutput, calls=%fused_computation.67.clone.1 | convolution fusion | flops 545260544 | bytes 10493956 | tf_op jit(solution)/shard_map/while/body/eval_jaxpr/sub | solution.py:46
  130.1 5.2 %fusion.71 = bf16[4,512,128]{1,2,0:T(8,128)(2,1)S(1)} fusion(bf16[1024,4,128]{0,2,1:T(8,128)(2,1)} %get-tuple-element.154, f32[4,512,1024]{2,1,0:T(8,128)} %get-tuple-element.127, f32[4,512]{1,0:T(4,128)S(1)} %get-tuple-element.128), kind=kOutput, calls=%fused_computation.11.clone.1 | convolution fusion | flops 541327360 | bytes 9969664 | tf_op jit(solution)/shard_map/while/body/eval_jaxpr/hqk,khd->qhd/dot_general | solution.py:48
  135.3 0.2 copy.84
  135.6 0.6 dynamic_slice.22
  136.9 0.4 iota_compare_fusion.5
  137.2 7.5 %fusion.70 = (f32[4,512]{1,0:T(4,128)S(1)}, f32[4,512,1024]{2,1,0:T(8,128)}) fusion(pred[512,1024]{1,0:T(8,128)(4,1)S(1)} %iota_compare_fusion.5, bf16[1024,4,128]{2,0,1:T(8,128)(2,1)S(1)} %get-tuple-element.153, bf16[1024,4,128]{0,2,1:T(8,128)(2,1)} %get-tuple-element.152, s32[]{:T(128)S(6)} %select_n.32), kind=kOutput, calls=%fused_computation.67.clone.1 | convolution fusion | flops 545260544 | bytes 10493956 | tf_op jit(solution)/shard_map/while/body/eval_jaxpr/sub | solution.py:46
  144.8 5.2 %fusion.71 = bf16[4,512,128]{1,2,0:T(8,128)(2,1)S(1)} fusion(bf16[1024,4,128]{0,2,1:T(8,128)(2,1)} %get-tuple-element.154, f32[4,512,1024]{2,1,0:T(8,128)} %get-tuple-element.127, f32[4,512]{1,0:T(4,128)S(1)} %get-tuple-element.128), kind=kOutput, calls=%fused_computation.11.clone.1 | convolution fusion | flops 541327360 | bytes 9969664 | tf_op jit(solution)/shard_map/while/body/eval_jaxpr/hqk,khd->qhd/dot_general | solution.py:48
  150.0 0.2 copy.84
  150.7 1.6 copy.82
  152.4 0.5 broadcast.146
  152.9 7.1 %reduce.4 = bf16[1024,512]{1,0:T(8,128)(2,1)S(1)} reduce(bf16[1024,1,512]{2,1,0:T(2,128)(2,1)S(1)} %bitcast.102, bf16[]{:T(256)} %broadcast.146), dimensions={1}, to_apply=%bitcast.88.reduce_sub_computation | reduce | bytes 2097154
  159.9 0.0 copy-start.2
  159.9 1.6 reshape.239
  161.5 3.6 all-to-all-start.1
  165.2 0.0 copy-done.4
  165.2 0.1 copy.62
  165.3 0.1 eq.40
  165.4 0.1 eq.44
  165.6 0.0 copy-done.2
  165.6 1.3 copy.61
  166.9 0.6 reduce-window.6
  167.5 0.2 slice_reduce_fusion
  167.7 0.1 fusion.46
  167.8 0.1 sub.17
  168.0 0.1 copy.66
  168.0 0.1 fusion.44
  168.1 23.0 %all-to-all-done.1 = bf16[8,2,32768]{2,1,0:T(2,128)(2,1)S(1)} async-done(((bf16[8,2,32768]{2,1,0:T(2,128)(2,1)}), bf16[8,2,32768]{2,1,0:T(2,128)(2,1)S(1)}, u32[]{:S(2)}, u32[]{:S(2)}) %all-to-all-start.1) | async-done | bytes 1048608 | tf_op jit(solution)/shard_map/all_to_all | solution.py:55
  191.1 1.0 reshape.240
  192.2 0.3 copy.74
  192.4 0.0 copy-start.3
  192.5 0.7 copy.60
  193.1 1.8 fusion.31
  195.0 0.0 copy-done.3
  195.0 0.0 slice-start
  195.0 1.7 convolution_convert_fusion
  196.7 0.0 slice-start.1
  196.7 97.1 %all_to_all.46 = bf16[32,16,4096]{2,1,0:T(8,128)(2,1)S(1)} all-to-all(bf16[32,16,4096]{2,1,0:T(8,128)(2,1)S(1)} %bitcast.97), channel_id=1, replica_groups=mesh['seq'=8,'exp'=4] {'seq','exp'}, dimensions={0} | all-to-all | bytes 8388608 | tf_op jit(solution)/shard_map/all_to_all | solution.py:78
  293.8 2.0 copy-done
  295.8 0.0 slice-done
  295.8 0.0 slice-done.1
  295.8 4.6 %fusion.26 = f32[512,768]{1,0:T(8,128)} fusion(bf16[512,4096]{1,0:T(8,128)(2,1)S(1)} %bitcast.105, bf16[1,4096,768]{2,1,0:T(8,128)(2,1)S(1)} %bitcast.114), kind=kOutput, calls=%fused_computation.26 | convolution fusion | flops 3221225472 | bytes 12058624 | tf_op jit(solution)/shard_map/dot_general | solution.py:12
  300.4 17.0 %fusion.28 = bf16[512,4096]{1,0:T(8,128)(2,1)} fusion(bf16[1,768,4096]{2,1,0:T(8,128)(2,1)} %param.17, f32[512,768]{1,0:T(8,128)} %fusion.26, bf16[512,4096]{1,0:T(8,128)(2,1)} %bitcast.106, bf16[1,4096,768]{2,1,0:T(8,128)(2,1)} %param.16), kind=kOutput, calls=%fused_computation.29 | convolution fusion | flops 6446907392 | bytes 22544384 | tf_op jit(solution)/shard_map/dot_general | solution.py:15
  317.4 4.0 all-to-all-start.3
  321.5 0.1 mul.106
  321.7 1.3 copy.69
  323.0 92.7 %all-to-all-done.3 = bf16[32,16,4096]{2,1,0:T(8,128)(2,1)} async-done(((bf16[32,16,4096]{2,1,0:T(8,128)(2,1)}), bf16[32,16,4096]{2,1,0:T(8,128)(2,1)}, u32[]{:S(2)}, u32[]{:S(2)}) %all-to-all-start.3) | async-done | bytes 4194336 | tf_op jit(solution)/shard_map/all_to_all | solution.py:83
  415.7 6.6 %gather_fusion = bf16[256,4096]{1,0:T(8,128)(2,1)S(1)} fusion(bf16[512,4096]{1,0:T(8,128)(2,1)} %bitcast.20, s32[1024]{0:T(1024)S(1)} %pad_clamp_fusion), kind=kCustom, calls=%fused_computation | custom fusion | bytes 4195328 | tf_op jit(solution)/shard_map/gather | solution.py:85
  422.3 4.0 reshape.229
  426.3 9.9 %fusion.54 = (f32[128,1,4096]{2,1,0:T(1,128)}, f32[128,1,4096]{2,1,0:T(1,128)}) fusion(f32[128,2,4096]{2,1,0:T(2,128)} %reshape.229), kind=kLoop, calls=%fused_computation.68 | loop fusion | bytes 8388608 | tf_op jit(solution)/shard_map/slice | solution.py:88
  436.1 5.0 %copy.76 = f32[128,1,4096]{0,2,1:T(8,128)S(1)} copy(f32[128,1,4096]{2,1,0:T(1,128)} %get-tuple-element.82) | data formatting | bytes 4194304
  441.2 5.6 %copy.75 = f32[128,1,4096]{0,2,1:T(8,128)} copy(f32[128,1,4096]{2,1,0:T(1,128)} %get-tuple-element.81) | data formatting | bytes 4194304
  446.8 3.0 fusion.34
  449.8 2.3 copy.70
  (24 shorter events, 0.2 us)
Async XLA Ops:
  7.8 100.6 %all-to-all-start = ((bf16[1,128,3,4096]{1,2,0,3:T(4,128)(2,1)}), bf16[1,128,3,4096]{1,2,0,3:T(4,128)(2,1)}, u32[]{:S(2)}, u32[]{:S(2)}) async-start(bf16[1,128,3,4096]{1,2,0,3:T(4,128)(2,1)} %copy.54), calls=%async_computation | async-start | bytes 8388608 | tf_op jit(solution)/shard_map/all_to_all | solution.py:24
  116.5 4.4 copy-start.1
  152.9 12.3 %copy-start.4 = (s32[1,128,2]{1,2,0:T(2,128)S(1)}, s32[1,128,2]{1,2,0:T(2,128)}, u32[]{:S(2)}) copy-start(s32[1,128,2]{1,2,0:T(2,128)} %param.13) | copy-start | bytes 3076
  159.9 5.6 %copy-start.2 = (bf16[1,128,4096]{2,1,0:T(8,128)(2,1)S(1)}, bf16[1,128,4096]{2,1,0:T(8,128)(2,1)}, u32[]{:S(2)}) copy-start(bf16[1,128,4096]{2,1,0:T(8,128)(2,1)} %param.11) | copy-start | bytes 3145732
  161.5 29.6 %all-to-all-start.1 = ((bf16[8,2,32768]{2,1,0:T(2,128)(2,1)}), bf16[8,2,32768]{2,1,0:T(2,128)(2,1)S(1)}, u32[]{:S(2)}, u32[]{:S(2)}) async-start(bf16[8,2,32768]{2,1,0:T(2,128)(2,1)} %reshape.239), calls=%async_computation.1 | async-start | bytes 2097152 | tf_op jit(solution)/shard_map/all_to_all | solution.py:55
  192.4 2.5 copy-start.3
  195.0 100.8 %slice-start = ((s8[6291456]{0:T(1024)(128)(4,1)}), s8[4194304]{0:T(1024)(128)(4,1)S(1)}, s32[]{:S(2)}) async-start(s8[6291456]{0:T(1024)(128)(4,1)} %bitcast.113), calls=%async_computation.4 | async-start | bytes 8388608
  196.7 99.1 %slice-start.1 = ((s8[6291456]{0:T(1024)(128)(4,1)}), s8[2097152]{0:T(1024)(128)(4,1)S(1)}, s32[]{:S(2)}) async-start(s8[6291456]{0:T(1024)(128)(4,1)} %bitcast.113), calls=%async_computation.5 | async-start | bytes 4194304
  293.8 2.0 copy-start
  317.4 4.2 copy-start.5
  317.4 98.2 %all-to-all-start.3 = ((bf16[32,16,4096]{2,1,0:T(8,128)(2,1)}), bf16[32,16,4096]{2,1,0:T(8,128)(2,1)}, u32[]{:S(2)}, u32[]{:S(2)}) async-start(bf16[32,16,4096]{2,1,0:T(8,128)(2,1)} %bitcast.104), calls=%async_computation.3 | async-start | bytes 8388608 | tf_op jit(solution)/shard_map/all_to_all | solution.py:83
where the time goes:
time: 460 us; the launch traced here: 452 us
  waiting for transfers between devices  209 us (45%)
  blocking collectives  97.1 us (21%)
  local copies, waits for them, and re-layouts  66 us (14%)
  matrix products  48.8 us (11%)
  starting transfers between devices  14.9 us (3%)
  other arithmetic  13.5 us (3%)
    all_to_all x1, blocking collectives, shards(): lax.all_to_all(outgoing, ('seq', 'exp'), split_axis=0, concat_axis=0, til...  97.1 us
    all_to_all x1, waiting for transfers between devices, shards(): lax.all_to_all(projected, 'seq', split_axis=3, concat_axis=1, tiled=True)  93.3 us
    all_to_all x1, waiting for transfers between devices, shards(): lax.all_to_all(processed, ('seq', 'exp'), split_axis=0, concat_axis=0, ti...  92.7 us
    unnamed x27, local copies, waits for them, and re-layouts  28.3 us
    all_to_all x1, waiting for transfers between devices, shards(): lax.all_to_all(head_major, 'seq', split_axis=1, concat_axis=2, tiled=True)  23 us
    dot_general x1, matrix products, expert_ffn(): jnp.dot(hidden, w_down[0], preferred_element_type=jnp.float32)  17 us
    sub x2, matrix products, attend(): weights = jnp.exp(scores - highest)  15.1 us
    dot_general x2, matrix products, attend(): jnp.einsum('hqk,khd->qhd', probs, value_rows, preferred_element_type=jnp....  10.4 us
  transfers between devices with their start and end apart: 3, of which 3 were waited for; matrix products, arithmetic and copies ran while one was open for 1% of the time, Pallas kernels for 0%

commit v1 on v0

--- a/solution.py
+++ b/solution.py
@@ -21,7 +21,15 @@
     exp_count = lax.axis_size("exp")
     tok_rows = patches.shape[1]
     width = patches.shape[2]
-    regrouped = lax.all_to_all(projected, "seq", split_axis=3, concat_axis=1, tiled=True)
+    ways, here = (lax.axis_size("seq"), lax.axis_index("seq"))
+    width_2 = projected.shape[3] // ways
+    turned = jnp.roll(projected, -here * width_2, axis=3)
+    got = [lax.slice_in_dim(turned, 0, width_2, axis=3)]
+    for far in range(1, ways):
+        sent = lax.slice_in_dim(turned, far * width_2, (far + 1) * width_2, axis=3)
+        got.append(lax.ppermute(sent, "seq", [(d, (d + far) % ways) for d in range(ways)]))
+    line = jnp.concatenate(got[::-1], axis=1)
+    regrouped = jnp.roll(line, (here + 1) * got[0].shape[1], axis=1)
     length = regrouped.shape[1]
     local_width = regrouped.shape[3]
     local_heads = HEADS // seq_count

time: 460 us -> 437 us (0.950)
  waiting for transfers between devices: 209 us -> 176 us
    all_to_all x1 -> x0, waiting for transfers between devices: 93.3 us -> none  [shards(): lax.all_to_all(projected, 'seq', split_axis=3, concat_axis=1, tiled=True)]
    ppermute x0 -> x7, waiting for transfers between devices: none -> 61.7 us  [shards(): lax.ppermute(sent, 'seq', [(d, (d + far) % ways) for d in range(ways)])]
    ppermute x0 -> x7, starting transfers between devices: none -> 9.5 us  [shards(): lax.ppermute(sent, 'seq', [(d, (d + far) % ways) for d in range(ways)])]
    unnamed x27 -> x38, local copies, waits for them, and re-layouts: 28.3 us -> 36.6 us
    all_to_all x2 -> x0, local copies, waits for them, and re-layouts: 8.12 us -> none  [shards(): lax.all_to_all(projected, 'seq', split_axis=3, concat_axis=1, tiled=True)]
    all_to_all x1 -> x0, starting transfers between devices: 7.28 us -> none  [shards(): lax.all_to_all(projected, 'seq', split_axis=3, concat_axis=1, tiled=True)]
  transfers between devices with their start and end apart: 3 -> 9, of which waited for: 3 -> 6; matrix products, arithmetic and copies ran while one was open for 1% -> 2% of each run, Pallas kernels for 0% -> 0%
where the time goes in v1:
time: 437 us; the launch traced here: 428 us
  waiting for transfers between devices  176 us (40%)
  blocking collectives  96.8 us (22%)
  local copies, waits for them, and re-layouts  69.4 us (16%)
  matrix products  49 us (11%)
  starting transfers between devices  17.1 us (4%)
  other arithmetic  16.9 us (4%)
    all_to_all x1, blocking collectives, shards(): lax.all_to_all(outgoing, ('seq', 'exp'), split_axis=0, concat_axis=0, til...  96.8 us
    all_to_all x1, waiting for transfers between devices, shards(): lax.all_to_all(processed, ('seq', 'exp'), split_axis=0, concat_axis=0, ti...  92.7 us
    ppermute x7, waiting for transfers between devices, shards(): lax.ppermute(sent, 'seq', [(d, (d + far) % ways) for d in range(ways)])  61.7 us
    unnamed x38, local copies, waits for them, and re-layouts  36.6 us
    all_to_all x1, waiting for transfers between devices, shards(): lax.all_to_all(head_major, 'seq', split_axis=1, concat_axis=2, tiled=True)  21.4 us
    dot_general x1, matrix products, expert_ffn(): jnp.dot(hidden, w_down[0], preferred_element_type=jnp.float32)  17 us
    sub x2, matrix products, attend(): weights = jnp.exp(scores - highest)  15.1 us
    dot_general x2, matrix products, attend(): jnp.einsum('hqk,khd->qhd', probs, value_rows, preferred_element_type=jnp....  10.6 us
  transfers between devices with their start and end apart: 9, of which 6 were waited for; matrix products, arithmetic and copies ran while one was open for 2% of the time, Pallas kernels for 0%

profile of v1, /device:TPU:0, one launch (start us, length us, event | category | flops | bytes accessed | tf_op | source)
XLA Modules:
  0.0 428.2 jit_solution(13934563700569808968)
XLA Ops:
  0.7 4.7 %copy.56 = bf16[1,128,3,4096]{1,3,2,0:T(8,128)(2,1)} copy(bf16[1,128,3,4096]{3,1,2,0:T(8,128)(2,1)} %param.10) | data formatting | bytes 6291456 | tf_op args[0]
  5.3 3.4 fusion.31
  8.7 1.6 fusion.56
  10.3 6.0 %collective-permute-start = (bf16[1,128,3,512]{1,3,2,0:T(8,128)(2,1)}, bf16[1,128,3,512]{1,3,2,0:T(8,128)(2,1)S(1)}, u32[]{:S(2)}, u32[]{:S(2)}) collective-permute-start(bf16[1,128,3,512]{1,3,2,0:T(8,128)(2,1)} %get-tuple-element.92), channel_id=1, source_target_pairs={{0,28},{4,0},{8,4},{12,8},{16,12},{20,16},{24,20},{28,24},{1,29},{... | collective-permute-start | bytes 1179656 | tf_op jit(solution)/shard_map/ppermute | solution.py:30
  16.3 0.4 collective-permute-start.1
  16.8 3.0 collective-permute-start.3
  19.8 6.4 %collective-permute-done = bf16[1,128,3,512]{1,3,2,0:T(8,128)(2,1)S(1)} collective-permute-done((bf16[1,128,3,512]{1,3,2,0:T(8,128)(2,1)}, bf16[1,128,3,512]{1,3,2,0:T(8,128)(2,1)S(1)}, u32[]{:S(2)}, u32[]{:S(2)}) %collective-permute-start) | collective-permute-done | bytes 393248 | tf_op jit(solution)/shard_map/ppermute | solution.py:30
  26.3 8.3 %collective-permute-done.1 = bf16[1,128,3,512]{1,3,2,0:T(8,128)(2,1)} collective-permute-done((bf16[1,128,3,512]{1,3,2,0:T(8,128)(2,1)}, bf16[1,128,3,512]{1,3,2,0:T(8,128)(2,1)}, u32[]{:S(2)}, u32[]{:S(2)}) %collective-permute-start.1) | collective-permute-done | bytes 393248 | tf_op jit(solution)/shard_map/ppermute | solution.py:30
  34.7 1.1 constant_dynamic-update-slice_fusion.13
  35.8 7.3 %collective-permute-done.2 = bf16[1,128,3,512]{1,3,2,0:T(8,128)(2,1)} collective-permute-done((bf16[1,128,3,512]{1,3,2,0:T(8,128)(2,1)}, bf16[1,128,3,512]{1,3,2,0:T(8,128)(2,1)}, u32[]{:S(2)}, u32[]{:S(2)}) %collective-permute-start.2) | collective-permute-done | bytes 393248 | tf_op jit(solution)/shard_map/ppermute | solution.py:30
  43.1 1.1 constant_dynamic-update-slice_fusion.12
  44.3 39.6 %collective-permute-done.3 = bf16[1,128,3,512]{1,3,2,0:T(8,128)(2,1)} collective-permute-done((bf16[1,128,3,512]{1,3,2,0:T(8,128)(2,1)}, bf16[1,128,3,512]{1,3,2,0:T(8,128)(2,1)}, u32[]{:S(2)}, u32[]{:S(2)}) %collective-permute-start.3) | collective-permute-done | bytes 393248 | tf_op jit(solution)/shard_map/ppermute | solution.py:30
  83.8 1.1 constant_dynamic-update-slice_fusion.11
  85.0 1.1 constant_dynamic-update-slice_fusion.10
  86.7 1.1 constant_dynamic-update-slice_fusion.6
  87.8 1.1 constant_dynamic-update-slice_fusion.5
  89.0 1.1 constant_dynamic-update-slice_fusion.4
  90.1 1.1 constant_dynamic-update-slice_fusion.3
  91.7 1.9 constant_dynamic-slice_fusion.2
  93.5 0.7 copy.59
  94.2 32.1 %while.10 = (s32[]{:T(128)}, bf16[2,512,512]{2,1,0:T(8,128)(2,1)}, s32[2]{0:T(128)S(1)}, bf16[1024,4,128]{0,2,1:T(8,128)(2,1)}, bf16[1024,4,128]{2,0,1:T(8,128)(...) while((s32[]{:T(128)}, bf16[2,512,512]{2,1,0:T(8,128)(2,1)}, ...), condition=%wide.region_3.4_spmd, body=%wide.region_0.3_spmd.sunk | while | flops 1087112704 | bytes 31477988 | solution.py:61
  94.2 0.7 dynamic_slice.40
  95.6 0.4 iota_compare_fusion.5
  96.0 7.5 %fusion.71 = (f32[4,512]{1,0:T(4,128)S(1)}, f32[4,512,1024]{2,1,0:T(8,128)}) fusion(pred[512,1024]{1,0:T(8,128)(4,1)S(1)} %iota_compare_fusion.5, bf16[1024,4,128]{2,0,1:T(8,128)(2,1)S(1)} %get-tuple-element.160, bf16[1024,4,128]{0,2,1:T(8,128)(2,1)} %get-tuple-element.159, s32[]{:T(128)S(6)} %select_n.59), kind=kOutput, calls=%fused_computation.88.clone.1 | convolution fusion | flops 545260544 | bytes 10493956 | tf_op jit(solution)/shard_map/while/body/eval_jaxpr/sub | solution.py:54
  103.5 5.3 %fusion.72 = bf16[4,512,128]{1,2,0:T(8,128)(2,1)S(1)} fusion(bf16[1024,4,128]{0,2,1:T(8,128)(2,1)} %get-tuple-element.161, f32[4,512,1024]{2,1,0:T(8,128)} %get-tuple-element.134, f32[4,512]{1,0:T(4,128)S(1)} %get-tuple-element.135), kind=kOutput, calls=%fused_computation.11.clone.1 | convolution fusion | flops 541327360 | bytes 9969664 | tf_op jit(solution)/shard_map/while/body/eval_jaxpr/hqk,khd->qhd/dot_general | solution.py:56
  108.8 0.2 copy.84
  109.1 1.0 copy-done.2
  110.1 0.7 dynamic_slice.40
  111.4 0.4 iota_compare_fusion.5
  111.8 7.5 %fusion.71 = (f32[4,512]{1,0:T(4,128)S(1)}, f32[4,512,1024]{2,1,0:T(8,128)}) fusion(pred[512,1024]{1,0:T(8,128)(4,1)S(1)} %iota_compare_fusion.5, bf16[1024,4,128]{2,0,1:T(8,128)(2,1)S(1)} %get-tuple-element.160, bf16[1024,4,128]{0,2,1:T(8,128)(2,1)} %get-tuple-element.159, s32[]{:T(128)S(6)} %select_n.59), kind=kOutput, calls=%fused_computation.88.clone.1 | convolution fusion | flops 545260544 | bytes 10493956 | tf_op jit(solution)/shard_map/while/body/eval_jaxpr/sub | solution.py:54
  119.4 5.3 %fusion.72 = bf16[4,512,128]{1,2,0:T(8,128)(2,1)S(1)} fusion(bf16[1024,4,128]{0,2,1:T(8,128)(2,1)} %get-tuple-element.161, f32[4,512,1024]{2,1,0:T(8,128)} %get-tuple-element.134, f32[4,512]{1,0:T(4,128)S(1)} %get-tuple-element.135), kind=kOutput, calls=%fused_computation.11.clone.1 | convolution fusion | flops 541327360 | bytes 9969664 | tf_op jit(solution)/shard_map/while/body/eval_jaxpr/hqk,khd->qhd/dot_general | solution.py:56
  124.7 0.2 copy.84
  125.0 1.0 copy-done.2
  126.4 2.8 copy.82
  129.2 0.5 broadcast.148
  129.7 7.0 %reduce.4 = bf16[1024,512]{1,0:T(8,128)(2,1)S(1)} reduce(bf16[1024,1,512]{2,1,0:T(2,128)(2,1)S(1)} %bitcast.93, bf16[]{:T(256)} %broadcast.148), dimensions={1}, to_apply=%bitcast.80.reduce_sub_computation | reduce | bytes 2097154
  136.8 1.6 reshape.239
  138.4 3.6 all-to-all-start
  142.1 0.1 eq.49
  142.2 0.1 eq.45
  142.3 2.3 copy.63
  144.6 0.6 reduce-window.6
  145.2 0.2 slice_reduce_fusion
  145.6 0.1 sub.27
  145.9 21.4 %all-to-all-done = bf16[8,2,32768]{2,1,0:T(2,128)(2,1)S(1)} async-done(((bf16[8,2,32768]{2,1,0:T(2,128)(2,1)}), bf16[8,2,32768]{2,1,0:T(2,128)(2,1)S(1)}, u32[]{:S(2)}, u32[]{:S(2)}) %all-to-all-start) | async-done | bytes 1048608 | tf_op jit(solution)/shard_map/all_to_all | solution.py:63
  167.2 1.0 reshape.240
  168.3 0.3 copy.76
  168.6 0.7 copy.62
  169.2 1.8 fusion.32
  171.1 1.7 convolution_convert_fusion
  172.8 96.8 %all_to_all.28 = bf16[32,16,4096]{2,1,0:T(8,128)(2,1)S(1)} all-to-all(bf16[32,16,4096]{2,1,0:T(8,128)(2,1)S(1)} %bitcast.89), channel_id=1, replica_groups=mesh['seq'=8,'exp'=4] {'seq','exp'}, dimensions={0} | all-to-all | bytes 8388608 | tf_op jit(solution)/shard_map/all_to_all | solution.py:86
  269.7 2.0 copy-done
  271.7 4.6 %fusion.26 = f32[512,768]{1,0:T(8,128)} fusion(bf16[512,4096]{1,0:T(8,128)(2,1)S(1)} %bitcast.96, bf16[1,4096,768]{2,1,0:T(8,128)(2,1)S(1)} %bitcast.104), kind=kOutput, calls=%fused_computation.28 | convolution fusion | flops 3221225472 | bytes 12058624 | tf_op jit(solution)/shard_map/dot_general | solution.py:12
  276.3 17.0 %fusion.28 = bf16[512,4096]{1,0:T(8,128)(2,1)} fusion(bf16[1,768,4096]{2,1,0:T(8,128)(2,1)} %param.17, f32[512,768]{1,0:T(8,128)} %fusion.26, bf16[512,4096]{1,0:T(8,128)(2,1)} %bitcast.97, bf16[1,4096,768]{2,1,0:T(8,128)(2,1)} %param.16), kind=kOutput, calls=%fused_computation.31 | convolution fusion | flops 6446907392 | bytes 22544384 | tf_op jit(solution)/shard_map/dot_general | solution.py:15
  293.3 4.0 all-to-all-start.2
  297.5 1.3 copy.71
  298.8 92.7 %all-to-all-done.2 = bf16[32,16,4096]{2,1,0:T(8,128)(2,1)} async-done(((bf16[32,16,4096]{2,1,0:T(8,128)(2,1)}), bf16[32,16,4096]{2,1,0:T(8,128)(2,1)}, u32[]{:S(2)}, u32[]{:S(2)}) %all-to-all-start.2) | async-done | bytes 4194336 | tf_op jit(solution)/shard_map/all_to_all | solution.py:91
  391.5 6.6 %gather_fusion = bf16[256,4096]{1,0:T(8,128)(2,1)S(1)} fusion(bf16[512,4096]{1,0:T(8,128)(2,1)} %bitcast.18, s32[1024]{0:T(1024)S(1)} %pad_clamp_fusion), kind=kCustom, calls=%fused_computation | custom fusion | bytes 4195328 | tf_op jit(solution)/shard_map/gather | solution.py:93
  398.1 4.0 reshape.229
  402.1 9.9 %fusion.55 = (f32[128,1,4096]{2,1,0:T(1,128)}, f32[128,1,4096]{2,1,0:T(1,128)}) fusion(f32[128,2,4096]{2,1,0:T(2,128)} %reshape.229), kind=kLoop, calls=%fused_computation.89 | loop fusion | bytes 8388608 | tf_op jit(solution)/shard_map/slice | solution.py:96
  412.0 5.0 %copy.77 = f32[128,1,4096]{0,2,1:T(8,128)S(1)} copy(f32[128,1,4096]{2,1,0:T(1,128)} %get-tuple-element.84) | data formatting | bytes 4194304
  417.0 5.6 %copy.78 = f32[128,1,4096]{0,2,1:T(8,128)} copy(f32[128,1,4096]{2,1,0:T(1,128)} %get-tuple-element.85) | data formatting | bytes 4194304
  422.7 3.0 fusion.35
  425.7 2.3 copy.72
  (56 shorter events, 1.8 us)
Async XLA Ops:
  10.3 15.9 %collective-permute-start = (bf16[1,128,3,512]{1,3,2,0:T(8,128)(2,1)}, bf16[1,128,3,512]{1,3,2,0:T(8,128)(2,1)S(1)}, u32[]{:S(2)}, u32[]{:S(2)}) collective-permute-start(bf16[1,128,3,512]{1,3,2,0:T(8,128)(2,1)} %get-tuple-element.92), channel_id=1, source_target_pairs={{0,28},{4,0},{8,4},{12,8},{16,12},{20,16},{24,20},{28,24},{1,29},{... | collective-permute-start | bytes 1179656 | tf_op jit(solution)/shard_map/ppermute | solution.py:30
  16.3 18.3 %collective-permute-start.1 = (bf16[1,128,3,512]{1,3,2,0:T(8,128)(2,1)}, bf16[1,128,3,512]{1,3,2,0:T(8,128)(2,1)}, u32[]{:S(2)}, u32[]{:S(2)}) collective-permute-start(bf16[1,128,3,512]{1,3,2,0:T(8,128)(2,1)} %get-tuple-element.91), channel_id=1, source_target_pairs={{0,24},{4,28},{8,0},{12,4},{16,8},{20,12},{24,16},{28,20},{1,25},{... | collective-permute-start | bytes 1179656 | tf_op jit(solution)/shard_map/ppermute | solution.py:30
  16.8 26.4 %collective-permute-start.2 = (bf16[1,128,3,512]{1,3,2,0:T(8,128)(2,1)}, bf16[1,128,3,512]{1,3,2,0:T(8,128)(2,1)}, u32[]{:S(2)}, u32[]{:S(2)}) collective-permute-start(bf16[1,128,3,512]{1,3,2,0:T(8,128)(2,1)} %get-tuple-element.90), channel_id=1, source_target_pairs={{0,20},{4,24},{8,28},{12,0},{16,4},{20,8},{24,12},{28,16},{1,21},{... | collective-permute-start | bytes 1179656 | tf_op jit(solution)/shard_map/ppermute | solution.py:30
  16.8 67.1 %collective-permute-start.3 = (bf16[1,128,3,512]{1,3,2,0:T(8,128)(2,1)}, bf16[1,128,3,512]{1,3,2,0:T(8,128)(2,1)}, u32[]{:S(2)}, u32[]{:S(2)}) collective-permute-start(bf16[1,128,3,512]{1,3,2,0:T(8,128)(2,1)} %get-tuple-element.89), channel_id=1, source_target_pairs={{0,16},{4,20},{8,24},{12,28},{16,0},{20,4},{24,8},{28,12},{1,17},{... | collective-permute-start | bytes 1179656 | tf_op jit(solution)/shard_map/ppermute | solution.py:30
  19.8 65.2 %collective-permute-start.4 = (bf16[1,128,3,512]{1,3,2,0:T(8,128)(2,1)}, bf16[1,128,3,512]{1,3,2,0:T(8,128)(2,1)}, u32[]{:S(2)}, u32[]{:S(2)}) collective-permute-start(bf16[1,128,3,512]{1,3,2,0:T(8,128)(2,1)} %get-tuple-element.88), channel_id=1, source_target_pairs={{0,12},{4,16},{8,20},{12,24},{16,28},{20,0},{24,4},{28,8},{1,13},{... | collective-permute-start | bytes 1179656 | tf_op jit(solution)/shard_map/ppermute | solution.py:30
  26.2 59.9 %collective-permute-start.5 = (bf16[1,128,3,512]{1,3,2,0:T(8,128)(2,1)}, bf16[1,128,3,512]{1,3,2,0:T(8,128)(2,1)S(1)}, u32[]{:S(2)}, u32[]{:S(2)}) collective-permute-start(bf16[1,128,3,512]{1,3,2,0:T(8,128)(2,1)} %get-tuple-element.87), channel_id=1, source_target_pairs={{0,8},{4,12},{8,16},{12,20},{16,24},{20,28},{24,0},{28,4},{1,9},{5... | collective-permute-start | bytes 1179656 | tf_op jit(solution)/shard_map/ppermute | solution.py:30
  34.7 51.6 %collective-permute-start.6 = (bf16[1,128,3,512]{1,3,2,0:T(8,128)(2,1)}, bf16[1,128,3,512]{1,3,2,0:T(8,128)(2,1)S(1)}, u32[]{:S(2)}, u32[]{:S(2)}) collective-permute-start(bf16[1,128,3,512]{1,3,2,0:T(8,128)(2,1)} %get-tuple-element.86), channel_id=1, source_target_pairs={{0,4},{4,8},{8,12},{12,16},{16,20},{20,24},{24,28},{28,0},{1,5},{5... | collective-permute-start | bytes 1179656 | tf_op jit(solution)/shard_map/ppermute | solution.py:30
  103.5 5.5 %copy-start.1 = (bf16[2,512,512]{2,1,0:T(8,128)(2,1)S(1)}, bf16[2,512,512]{2,1,0:T(8,128)(2,1)}, u32[]{:S(2)}) copy-start(bf16[2,512,512]{2,1,0:T(8,128)(2,1)} %get-tuple-element.147) | copy-start | bytes 3145732 | tf_op jit(solution)/shard_map/while
  109.1 1.0 copy-start.2
  119.4 5.5 %copy-start.1 = (bf16[2,512,512]{2,1,0:T(8,128)(2,1)S(1)}, bf16[2,512,512]{2,1,0:T(8,128)(2,1)}, u32[]{:S(2)}) copy-start(bf16[2,512,512]{2,1,0:T(8,128)(2,1)} %get-tuple-element.147) | copy-start | bytes 3145732 | tf_op jit(solution)/shard_map/while
  124.9 1.0 copy-start.2
  126.4 15.6 %copy-start.4 = (s32[1,128,2]{1,2,0:T(2,128)S(1)}, s32[1,128,2]{1,2,0:T(2,128)}, u32[]{:S(2)}) copy-start(s32[1,128,2]{1,2,0:T(2,128)} %param.13) | copy-start | bytes 3076
  138.4 28.9 %all-to-all-start = ((bf16[8,2,32768]{2,1,0:T(2,128)(2,1)}), bf16[8,2,32768]{2,1,0:T(2,128)(2,1)S(1)}, u32[]{:S(2)}, u32[]{:S(2)}) async-start(bf16[8,2,32768]{2,1,0:T(2,128)(2,1)} %reshape.239), calls=%async_computation | async-start | bytes 2097152 | tf_op jit(solution)/shard_map/all_to_all | solution.py:63
  144.6 26.5 %copy-start.3 = (f32[4096]{0:T(1024)S(1)}, f32[4096]{0:T(1024)}, u32[]{:S(2)}) copy-start(f32[4096]{0:T(1024)} %param.12) | copy-start | bytes 49156
  171.1 100.5 %slice-start = ((s8[6291456]{0:T(1024)(128)(4,1)}), s8[4194304]{0:T(1024)(128)(4,1)S(1)}, s32[]{:S(2)}) async-start(s8[6291456]{0:T(1024)(128)(4,1)} %bitcast.103), calls=%async_computation.3 | async-start | bytes 8388608
  172.8 98.8 %slice-start.1 = ((s8[6291456]{0:T(1024)(128)(4,1)}), s8[2097152]{0:T(1024)(128)(4,1)S(1)}, s32[]{:S(2)}) async-start(s8[6291456]{0:T(1024)(128)(4,1)} %bitcast.103), calls=%async_computation.4 | async-start | bytes 4194304
  269.7 2.0 copy-start
  293.3 4.2 copy-start.5
  293.3 98.2 %all-to-all-start.2 = ((bf16[32,16,4096]{2,1,0:T(8,128)(2,1)}), bf16[32,16,4096]{2,1,0:T(8,128)(2,1)}, u32[]{:S(2)}, u32[]{:S(2)}) async-start(bf16[32,16,4096]{2,1,0:T(8,128)(2,1)} %bitcast.95), calls=%async_computation.2 | async-start | bytes 8388608 | tf_op jit(solution)/shard_map/all_to_all | solution.py:91
